TPU v7x, 32 devices: a whole 2x2x4 slice. The times are simulated.
32 devices in a mesh: rep: 2 (over x), node: 16 (over z, y, core).
Axes of the slice: x: 2, y: 2, z: 4, core: 2. Of those that a mesh axis runs over, the one named last changes fastest.
Arguments:
- tokens: bfloat16 [4096, 7168], P(('rep', 'node')), parts along dimension 0, may hold values from -6 to 6
- group_choice: int32 [4096, 4], P(('rep', 'node')), parts along dimension 0, may hold values from 0 to 7, as said below
- expert_picks: int32 [4096, 8], P(('rep', 'node')), parts along dimension 0, may hold values from 0 to 255, as said below
- gate_fixed: int32 [4096, 8], P(('rep', 'node')), parts along dimension 0, may hold values from 1 to 65535
- token_counts: int32 [32], P(('rep', 'node')), parts along dimension 0, may hold values from 16 to 128, as said below
- expert_gate: bfloat16 [7168, 2048], P(None, 'node'), may hold values from -0.0625 to 0.0625
- expert_up: bfloat16 [7168, 2048], P(None, 'node'), may hold values from -0.0625 to 0.0625
- expert_down: bfloat16 [2048, 7168], P('node'), may hold values from -0.1875 to 0.1875
Outputs:
- routed_out: bfloat16 [4096, 7168], P(('rep', 'node')), parts along dimension 0
There are 2 independent parts, one for each index of `rep`. A program takes and returns all parts, laid end to end along the dimension named above; an argument that names none is the same for every part. Nothing has to cross between parts.
Inputs may be any that keep to these rules, and one draw needn't show every extreme that they name: `group_choice`: each row holds 4 different groups. `expert_picks`: each row names 8 different experts, two from each group of the same row of group_choice (expert e lies in group e // 32); at most one of them is a held expert f * 32 with f < 2. Among the valid tokens of one device each held expert is picked at most 8 times, and in every draw one held expert is picked exactly 8 times on every device. `token_counts`: some device has 128 valid tokens and some device 2 * 8.
All inputs are finite; a program needn't handle non-finite values.
Results may differ from a plain program's by a relative error of at most 0.0064.
Values may be sent and summed in bfloat16 or wider, within the bound.
No kernel may reach another device: no remote copies, remote signals or barrier semaphores. Data moves between devices by JAX's collectives and lax.ppermute only.
A program may use at most 64 MiB of HBM per device.

v0:
```python
import jax
import jax.numpy as jnp
from jax import lax
from jax.sharding import PartitionSpec as P

SPLIT = 8
GROUP_SIZE = 32


def expert_partial(rows_in, expert_gate, expert_up, expert_down):
    shape_in = rows_in.shape
    flat_rows = rows_in.reshape(-1, shape_in[-1])
    gate_val = jnp.dot(flat_rows, expert_gate, preferred_element_type=jnp.float32)
    up_val = jnp.dot(flat_rows, expert_up, preferred_element_type=jnp.float32)
    hidden = (jax.nn.silu(gate_val) * up_val).astype(jnp.bfloat16)
    partial_out = jnp.dot(hidden, expert_down, preferred_element_type=jnp.float32).astype(
        jnp.bfloat16
    )
    return partial_out.reshape(shape_in[:-1] + (expert_down.shape[1],))


def local(
    tokens,
    group_choice,
    expert_picks,
    gate_fixed,
    token_counts,
    expert_gate,
    expert_up,
    expert_down,
):
    devices = lax.axis_size("node")
    flight = devices // SPLIT
    row_count = tokens.shape[0]
    capacity = row_count // 16
    positions = jnp.arange(row_count, dtype=jnp.int32)
    is_valid = positions < token_counts[0]
    gate_vals = gate_fixed.astype(jnp.float32)
    weight = 2.5 * gate_vals / jnp.sum(gate_vals, axis=1, keepdims=True)
    in_group = jnp.any((expert_picks // GROUP_SIZE)[:, :, None] == group_choice[:, None, :], axis=2)
    counted = in_group & is_valid[:, None]
    targets = jnp.arange(flight, dtype=jnp.int32) * GROUP_SIZE
    matches = counted[:, :, None] & (expert_picks[:, :, None] == targets[None, None, :])
    picked = jnp.any(matches, axis=1)
    shares = jnp.sum(jnp.where(matches, weight[:, :, None], 0.0), axis=1)
    slot_of = jnp.cumsum(picked.astype(jnp.int32), axis=0) - 1
    slot_ids = jnp.arange(capacity, dtype=jnp.int32)
    slot_hit = picked.T[:, None, :] & (slot_of.T[:, None, :] == slot_ids[None, :, None])
    source_row = jnp.sum(jnp.where(slot_hit, positions[None, None, :], 0), axis=2)
    slot_used = jnp.any(slot_hit, axis=2)
    outgoing = jnp.where(
        slot_used[:, :, None], jnp.take(tokens, source_row, axis=0), jnp.zeros((), jnp.bfloat16)
    )
    copies = jnp.repeat(outgoing, SPLIT, axis=0)
    returned = lax.all_to_all(
        expert_partial(
            lax.all_to_all(copies, "node", split_axis=0, concat_axis=0, tiled=True),
            expert_gate,
            expert_up,
            expert_down,
        ),
        "node",
        split_axis=0,
        concat_axis=0,
        tiled=True,
    )
    summed = jnp.sum(
        returned.reshape((flight, SPLIT) + returned.shape[1:]), axis=1, dtype=jnp.float32
    )
    expert_out = summed.astype(jnp.bfloat16)
    result = jnp.zeros((row_count, tokens.shape[1]), jnp.float32)
    for expert in range(flight):
        rows_back = jnp.take(
            expert_out[expert], jnp.clip(slot_of[:, expert], 0, capacity - 1), axis=0
        )
        result = result + shares[:, expert : expert + 1] * rows_back.astype(jnp.float32)
    return result.astype(jnp.bfloat16)


def solution(mesh):
    return jax.shard_map(
        local,
        mesh=mesh,
        in_specs=(
            P(("rep", "node"), None),
            P(("rep", "node"), None),
            P(("rep", "node"), None),
            P(("rep", "node"), None),
            P(("rep", "node")),
            P(None, "node"),
            P(None, "node"),
            P("node", None),
        ),
        out_specs=P(("rep", "node"), None),
        check_vma=False,
    )
```

profile of v0, /device:TPU:13, one launch (start us, length us, event | category | flops | bytes accessed | tf_op | source)
XLA Modules:
  0.0 120.8 jit_solution(17459301770604360620)
XLA Ops:
  0.0 0.0 copy-start
  0.8 0.7 add_select_fusion
  1.5 0.7 compare_reduce_fusion
  2.2 0.8 fusion.24
  3.0 0.1 copy.21
  3.1 0.2 reduce_window_sum.11
  3.3 0.1 copy.22
  3.3 0.2 fusion.23
  3.5 0.2 select_reduce_fusion
  3.7 0.1 reshape.96
  3.8 2.6 %gather_fusion = bf16[16,7168]{1,0:T(8,128)(2,1)S(1)} fusion(bf16[128,7168]{1,0:T(8,128)(2,1)} %param.10, s32[1024]{0:T(1024)S(1)} %pad_clamp_fusion.2), kind=kCustom, calls=%fused_computation.2 | custom fusion | bytes 458816 | tf_op jit(solution)/shard_map/jit(_take)/gather | solution.py:52
  6.4 0.1 fusion.13
  6.5 0.2 broadcast_in_dim.79
  6.7 0.0 copy-start.2
  6.7 48.1 %all_to_all.10 = bf16[16,8,7168]{2,1,0:T(8,128)(2,1)S(1)} all-to-all(bf16[16,8,7168]{2,1,0:T(8,128)(2,1)S(1)} %bitcast.40), channel_id=1, replica_groups=mesh['rep'=2,'node'=16] {'node'}, dimensions={0} | all-to-all | bytes 3670016 | tf_op jit(solution)/shard_map/all_to_all | solution.py:57
  54.8 0.0 copy-start.1
  54.8 1.2 %copy-done.1 = bf16[16,8,7168]{2,1,0:T(8,128)(2,1)} copy-done((bf16[16,8,7168]{2,1,0:T(8,128)(2,1)}, bf16[16,8,7168]{2,1,0:T(8,128)(2,1)S(1)}, u32[]{:S(2)}) %copy-start.1) | copy-done | bytes 1835032
  56.0 0.0 copy-done.2
  56.0 0.6 fusion.3
  56.7 0.0 copy-done
  56.7 4.5 %fusion = bf16[16,8,7168]{2,1,0:T(8,128)(2,1)} fusion(bf16[128,7168]{1,0:T(8,128)(2,1)S(1)} %copy-done, bf16[7168,128]{1,0:T(8,128)(2,1)} %param.16, bf16[16,8,7168]{2,1,0:T(8,128)(2,1)} %copy-done.1, f32[128,128]{1,0:T(8,128)S(1)} %fusion.3), kind=kOutput, calls=%fused_computation.4 | convolution fusion | flops 470777856 | bytes 7405568 | tf_op jit(solution)/shard_map/dot_general | solution.py:16
  61.2 0.0 copy-start.4
  61.2 0.0 copy-start.3
  61.2 5.3 %all-to-all-start.1 = ((bf16[16,8,7168]{2,1,0:T(8,128)(2,1)}), bf16[16,8,7168]{2,1,0:T(8,128)(2,1)}, u32[]{:S(2)}, u32[]{:S(2)}) async-start(bf16[16,8,7168]{2,1,0:T(8,128)(2,1)} %fusion), calls=%async_computation.1 | async-start | bytes 3670016 | tf_op jit(solution)/shard_map/all_to_all | solution.py:55
  66.5 0.2 fusion.15
  66.8 0.0 copy-done.4
  66.8 0.0 copy-done.3
  66.8 0.1 select_reduce_fusion.1
  66.9 41.5 %all-to-all-done.1 = bf16[16,8,7168]{2,1,0:T(8,128)(2,1)} async-done(((bf16[16,8,7168]{2,1,0:T(8,128)(2,1)}), bf16[16,8,7168]{2,1,0:T(8,128)(2,1)}, u32[]{:S(2)}, u32[]{:S(2)}) %all-to-all-start.1) | async-done | bytes 1835040 | tf_op jit(solution)/shard_map/all_to_all | solution.py:55
  108.5 1.7 %bitcast_reduce_fusion = bf16[2,8,7168]{2,1,0:T(8,128)(2,1)S(1)} fusion(bf16[16,8,7168]{2,1,0:T(8,128)(2,1)} %all-to-all-done.1), kind=kLoop, calls=%fused_computation.6 | loop fusion | flops 802816 | bytes 2064384 | tf_op jit(solution)/shard_map/reduce_sum | solution.py:67
  110.2 3.0 %gather_fusion.1 = bf16[128,7168]{1,0:T(8,128)(2,1)} fusion(bf16[8,7168]{1,0:T(8,128)(2,1)S(1)} %get-tuple-element.8, s32[1024]{0:T(1024)S(1)} %pad_clamp_fusion.1), kind=kCustom, calls=%fused_computation.clone | custom fusion | bytes 3670528 | tf_op jit(solution)/shard_map/jit(_take)/gather | solution.py:73
  113.2 2.9 %gather_fusion.2 = bf16[128,7168]{1,0:T(8,128)(2,1)} fusion(bf16[8,7168]{1,0:T(8,128)(2,1)S(1)} %get-tuple-element.9, s32[1024]{0:T(1024)S(1)} %pad_clamp_fusion), kind=kCustom, calls=%fused_computation.1.clone | custom fusion | bytes 3670528 | tf_op jit(solution)/shard_map/jit(_take)/gather | solution.py:73
  116.1 4.7 %add_convert_fusion = bf16[128,7168]{1,0:T(8,128)(2,1)} fusion(bf16[128,7168]{1,0:T(8,128)(2,1)} %gather_fusion.2, bf16[128,7168]{1,0:T(8,128)(2,1)} %gather_fusion.1, f32[128]{0:T(128)S(1)} %get-tuple-element.13, f32[128]{0:T(128)S(1)} %get-tuple-element.12, pred[128]{0:T(512)(128)(4,1)S(1)} %get-tuple-element.16, pred[128]{0:T(512)(128)(4,1)S(1)} %get-tuple-element.17), kind=kLoop, calls=%fused_computation.5 | loop fusion | flops 7340032 | bytes 5506304 | tf_op jit(solution)/shard_map/convert_element_type | solution.py:77
  (16 shorter events, 0.1 us)
Async XLA Ops:
  0.0 56.7 %copy-start = (bf16[128,7168]{1,0:T(8,128)(2,1)S(1)}, bf16[128,7168]{1,0:T(8,128)(2,1)}, u32[]{:S(2)}) copy-start(bf16[128,7168]{1,0:T(8,128)(2,1)} %param.17) | copy-start | bytes 5505028
  6.7 49.4 %copy-start.2 = (bf16[7168,128]{1,0:T(8,128)(2,1)S(1)}, bf16[7168,128]{1,0:T(8,128)(2,1)}, u32[]{:S(2)}) copy-start(bf16[7168,128]{1,0:T(8,128)(2,1)} %param.15) | copy-start | bytes 5505028
  54.8 1.2 %copy-start.1 = (bf16[16,8,7168]{2,1,0:T(8,128)(2,1)}, bf16[16,8,7168]{2,1,0:T(8,128)(2,1)S(1)}, u32[]{:S(2)}) copy-start(bf16[16,8,7168]{2,1,0:T(8,128)(2,1)S(1)} %all_to_all.10) | copy-start | bytes 5505028
  61.2 5.6 %copy-start.4 = (s32[128,8]{0,1:T(8,128)S(1)}, s32[128,8]{0,1:T(8,128)}, u32[]{:S(2)}) copy-start(s32[128,8]{0,1:T(8,128)} %param.13) | copy-start | bytes 12292
  61.2 5.6 %copy-start.3 = (s32[128,8]{0,1:T(8,128)S(1)}, s32[128,8]{0,1:T(8,128)}, u32[]{:S(2)}) copy-start(s32[128,8]{0,1:T(8,128)} %param.12) | copy-start | bytes 12292
  61.2 47.3 %all-to-all-start.1 = ((bf16[16,8,7168]{2,1,0:T(8,128)(2,1)}), bf16[16,8,7168]{2,1,0:T(8,128)(2,1)}, u32[]{:S(2)}, u32[]{:S(2)}) async-start(bf16[16,8,7168]{2,1,0:T(8,128)(2,1)} %fusion), calls=%async_computation.1 | async-start | bytes 3670016 | tf_op jit(solution)/shard_map/all_to_all | solution.py:55
where the time goes:
time: 121 us
  blocking collectives  48.1 us (40%)
  waiting for transfers between devices  41.5 us (34%)
  local copies, waits for them, and re-layouts  10.2 us (8%)
  other arithmetic  9.53 us (8%)
  starting transfers between devices  5.34 us (4%)
  matrix products  5.13 us (4%)
    all_to_all x1, blocking collectives, local(): lax.all_to_all(copies, 'node', split_axis=0, concat_axis=0, tiled=True)  48.1 us
    all_to_all x1, waiting for transfers between devices, local(): lax.all_to_all(expert_partial(lax.all_to_all(copies, 'node', split_axis=0...  41.5 us
    gather x2, local copies, waits for them, and re-layouts, local(): jnp.take(expert_out[expert], jnp.clip(slot_of[:, expert], 0, capacity - 1...  5.89 us
    all_to_all x1, starting transfers between devices, local(): lax.all_to_all(expert_partial(lax.all_to_all(copies, 'node', split_axis=0...  5.34 us
    convert_element_type x1, other arithmetic, local(): return result.astype(jnp.bfloat16)  4.66 us
    dot_general x1, matrix products, expert_partial(): jnp.dot(hidden, expert_down, preferred_element_type=jnp.float32)  4.5 us
    gather x1, local copies, waits for them, and re-layouts, local(): jnp.take(tokens, source_row, axis=0)  2.63 us
  transfers between devices with their start and end apart: 1, of which 1 were waited for; matrix products, arithmetic and copies ran while one was open for 0% of the time, Pallas kernels for 0%

commit v1 on v0

v1 whole, which is shorter than its diff:
```python
import functools

import jax
import jax.numpy as jnp
from jax import lax
from jax.experimental import pallas as pl
from jax.experimental.pallas import tpu as pltpu
from jax.sharding import PartitionSpec as P

SPLIT = 8
GROUP_SIZE = 32
SCALE = 2.5
CORES = 2
CHIPS = SPLIT // CORES

VMEM = pl.BlockSpec(memory_space=pltpu.VMEM)
SMEM = pl.BlockSpec(memory_space=pltpu.SMEM)
ANY = pl.BlockSpec(memory_space=pl.ANY)


def column_step(width, limit):
    step = limit
    while width % step:
        step -= 128
    return step


def route_kernel(
    flight,
    capacity,
    me_ref,
    count_ref,
    groups_ref,
    picks_ref,
    gate_ref,
    tokens_ref,
    *refs,
):
    row_refs = refs[:flight]
    select_ref, share_ref, held, sem = refs[flight:]
    load = pltpu.make_async_copy(tokens_ref, held, sem)
    load.start()
    picks = picks_ref[...]
    groups = groups_ref[...]
    row_count = picks.shape[1]
    lanes = lax.broadcasted_iota(jnp.int32, (1, row_count), 1)
    picked_group = lax.shift_right_logical(picks, GROUP_SIZE.bit_length() - 1)
    counted = picked_group == groups[0:1, :]
    for place in range(1, groups.shape[0]):
        counted = counted | (picked_group == groups[place : place + 1, :])
    counted = counted & (lanes < count_ref[0])
    gate_vals = gate_ref[...].astype(jnp.float32)
    weight = SCALE * gate_vals / jnp.sum(gate_vals, axis=0, keepdims=True)
    rows_of = lax.broadcasted_iota(jnp.int32, (row_count, row_count), 0)
    cols_of = lax.broadcasted_iota(jnp.int32, (row_count, row_count), 1)
    upto = (rows_of <= cols_of).astype(jnp.bfloat16)
    slots = lax.broadcasted_iota(jnp.int32, (capacity, row_count), 0)
    selects = []
    for step in range(flight):
        expert = lax.rem(me_ref[0] + step, flight)
        match = counted & (picks == expert * GROUP_SIZE)
        picked = jnp.max(match.astype(jnp.float32), axis=0, keepdims=True)
        share = jnp.sum(jnp.where(match, weight, 0.0), axis=0, keepdims=True)
        rank = jnp.dot(
            jnp.broadcast_to(picked, (capacity, row_count)).astype(jnp.bfloat16),
            upto,
            preferred_element_type=jnp.float32,
        )
        hit = (picked > 0.5) & (rank.astype(jnp.int32) - 1 == slots)
        selects.append(jnp.where(hit, 1.0, 0.0))
        slot_share = jnp.sum(jnp.where(hit, share, 0.0), axis=1, keepdims=True)
        share_ref[step * capacity : (step + 1) * capacity, :] = jnp.broadcast_to(
            slot_share, (capacity, share_ref.shape[1])
        )
    select = jnp.concatenate(selects, axis=0).astype(jnp.bfloat16)
    select_ref[...] = select
    load.wait()
    width = held.shape[1]
    span = column_step(width, 1024)
    for start in range(0, width, span):
        rows = jnp.dot(
            select, held[:, start : start + span], preferred_element_type=jnp.float32
        ).astype(jnp.bfloat16)
        for step in range(flight):
            row_refs[step][:, start : start + span] = rows[
                step * capacity : (step + 1) * capacity
            ]


def route(me, counts, groups, picks, gate, tokens, flight, capacity):
    row_count, width = tokens.shape
    return pl.pallas_call(
        functools.partial(route_kernel, flight, capacity),
        out_shape=[jax.ShapeDtypeStruct((capacity, width), jnp.bfloat16)] * flight
        + [
            jax.ShapeDtypeStruct((flight * capacity, row_count), jnp.bfloat16),
            jax.ShapeDtypeStruct((flight * capacity, 128), jnp.float32),
        ],
        in_specs=[SMEM, SMEM, VMEM, VMEM, VMEM, ANY],
        out_specs=[VMEM] * (flight + 2),
        scratch_shapes=[
            pltpu.VMEM((row_count, width), jnp.bfloat16),
            pltpu.SemaphoreType.DMA,
        ],
        compiler_params=pltpu.CompilerParams(vmem_limit_bytes=16 << 20),
        cost_estimate=pl.CostEstimate(
            flops=2 * flight * capacity * row_count * width,
            bytes_accessed=2 * row_count * width,
            transcendentals=0,
        ),
        name="route",
    )(me, counts, groups, picks, gate, tokens)


def ffn_kernel(blocks, *refs):
    in_refs = refs[:blocks]
    gate_refs = refs[blocks : blocks + CORES]
    up_refs = refs[blocks + CORES : blocks + 2 * CORES]
    down_refs = refs[blocks + 2 * CORES : blocks + 3 * CORES]
    out_refs = refs[blocks + 3 * CORES :]
    rows, width = in_refs[0].shape
    hid = gate_refs[0].shape[1]
    span = column_step(width, 1024)
    totals = [jnp.zeros((blocks * rows, 2 * hid), jnp.float32)] * CORES
    for start in range(0, width, span):
        part = slice(start, start + span)
        x = jnp.concatenate([ref[:, part] for ref in in_refs], axis=0)
        for core in range(CORES):
            both = jnp.concatenate([gate_refs[core][part, :], up_refs[core][part, :]], axis=1)
            totals[core] = totals[core] + jnp.dot(x, both, preferred_element_type=jnp.float32)
    hidden = []
    for total in totals:
        gate_val, up_val = total[:, :hid], total[:, hid:]
        hidden.append((gate_val / (1.0 + jnp.exp(-gate_val)) * up_val).astype(jnp.bfloat16))
    hidden = jnp.concatenate(hidden, axis=1)
    for start in range(0, width, span):
        part = slice(start, start + span)
        down = jnp.concatenate([ref[:, part] for ref in down_refs], axis=0)
        out = jnp.dot(hidden, down, preferred_element_type=jnp.float32).astype(jnp.bfloat16)
        for block in range(blocks):
            out_refs[block][:, part] = out[block * rows : (block + 1) * rows]


def ffn(xs, gates, ups, downs):
    blocks = len(xs)
    rows, width = xs[0].shape
    hid = gates[0].shape[1]
    return pl.pallas_call(
        functools.partial(ffn_kernel, blocks),
        out_shape=[jax.ShapeDtypeStruct((rows, width), jnp.bfloat16)] * blocks,
        in_specs=[VMEM] * (blocks + 3 * CORES),
        out_specs=[VMEM] * blocks,
        compiler_params=pltpu.CompilerParams(vmem_limit_bytes=30 << 20),
        cost_estimate=pl.CostEstimate(
            flops=2 * blocks * rows * width * hid * 3 * CORES,
            bytes_accessed=2 * 3 * CORES * width * hid,
            transcendentals=0,
        ),
        name="ffn",
    )(*xs, *gates, *ups, *downs)


def finish_kernel(flight, capacity, select_ref, share_ref, *refs):
    near_refs = refs[:CHIPS]
    far_refs = refs[CHIPS : CHIPS + flight - 1]
    out_ref, held, sems = refs[CHIPS + flight - 1 :]
    width = held.shape[1]
    span = column_step(width, 1024)
    select = select_ref[...]
    copies = []
    for place, start in enumerate(range(0, width, span)):
        part = slice(start, start + span)
        near = near_refs[0][:, part].astype(jnp.float32)
        for ref in near_refs[1:]:
            near = near + ref[:, part].astype(jnp.float32)
        near = near.astype(jnp.bfloat16).astype(jnp.float32)
        far = [ref[:, part].astype(jnp.float32) for ref in far_refs]
        rows = jnp.concatenate([near] + far, axis=0)
        scaled = (rows * share_ref[:, 0:1]).astype(jnp.bfloat16)
        held[:, part] = lax.dot_general(
            select, scaled, (((0,), (0,)), ((), ())), preferred_element_type=jnp.float32
        ).astype(jnp.bfloat16)
        copy = pltpu.make_async_copy(held.at[:, part], out_ref.at[:, part], sems.at[place])
        copy.start()
        copies.append(copy)
    for copy in copies:
        copy.wait()


def finish(select, share, nears, fars, capacity):
    flight = len(fars) + 1
    width = nears[0].shape[1]
    row_count = select.shape[1]
    places = width // column_step(width, 1024)
    return pl.pallas_call(
        functools.partial(finish_kernel, flight, capacity),
        out_shape=jax.ShapeDtypeStruct((row_count, width), jnp.bfloat16),
        in_specs=[VMEM] * (2 + len(nears) + len(fars)),
        out_specs=ANY,
        scratch_shapes=[
            pltpu.VMEM((row_count, width), jnp.bfloat16),
            pltpu.SemaphoreType.DMA((places,)),
        ],
        compiler_params=pltpu.CompilerParams(vmem_limit_bytes=16 << 20),
        cost_estimate=pl.CostEstimate(
            flops=2 * flight * capacity * row_count * width,
            bytes_accessed=2 * row_count * width,
            transcendentals=0,
        ),
        name="finish",
    )(select, share, *nears, *fars)


def local(
    tokens,
    group_choice,
    expert_picks,
    gate_fixed,
    token_counts,
    expert_gate,
    expert_up,
    expert_down,
):
    devices = lax.axis_size("node")
    flight = devices // SPLIT
    row_count = tokens.shape[0]
    capacity = row_count // 16
    me = (lax.axis_index("node") // SPLIT).astype(jnp.int32).reshape(1)

    def swap(array, bits):
        return lax.ppermute(array, "node", [(n, n ^ bits) for n in range(devices)])

    def shift(array, step):
        return lax.ppermute(
            array, "node", [(n, (n + step * SPLIT) % devices) for n in range(devices)]
        )

    gates = [expert_gate, swap(expert_gate, 1)]
    ups = [expert_up, swap(expert_up, 1)]
    downs = [expert_down, swap(expert_down, 1)]

    *rows, select, share = route(
        me, token_counts, group_choice.T, expert_picks.T, gate_fixed.T, tokens, flight, capacity
    )
    near = rows[0]
    far = [shift(rows[step], step) for step in range(1, flight)]
    far = far[0] if flight == 2 else jnp.concatenate(far, axis=0)

    nears = [near] + [swap(near, chip * CORES) for chip in range(1, CHIPS)]
    fars = [far] + [swap(far, chip * CORES) for chip in range(1, CHIPS)]

    near_parts = ffn(nears, gates, ups, downs)
    far_parts = ffn(fars, gates, ups, downs)

    far_back = [far_parts[0]] + [
        swap(far_parts[chip], chip * CORES) for chip in range(1, CHIPS)
    ]
    far_sum = far_back[0].astype(jnp.float32)
    for part in far_back[1:]:
        far_sum = far_sum + part.astype(jnp.float32)
    far_sum = far_sum.astype(jnp.bfloat16)
    far_home = [
        shift(far_sum[(step - 1) * capacity : step * capacity], -step)
        for step in range(1, flight)
    ]
    near_back = [near_parts[0]] + [
        swap(near_parts[chip], chip * CORES) for chip in range(1, CHIPS)
    ]
    return finish(select, share, near_back, far_home, capacity)


def solution(mesh):
    return jax.shard_map(
        local,
        mesh=mesh,
        in_specs=(
            P(("rep", "node"), None),
            P(("rep", "node"), None),
            P(("rep", "node"), None),
            P(("rep", "node"), None),
            P(("rep", "node")),
            P(None, "node"),
            P(None, "node"),
            P("node", None),
        ),
        out_specs=P(("rep", "node"), None),
        check_vma=False,
    )
```

time: 121 us -> 56.8 us (0.47)
  the two profiles are of different devices: /device:TPU:13 before, /device:TPU:0 now
where the time goes in v1:
time: 56.8 us; the launch traced here: 56.5 us
  starting transfers between devices  21.6 us (38%)
  waiting for transfers between devices  15.7 us (28%)
  Pallas kernels  11.8 us (21%)
  local copies, waits for them, and re-layouts  6.55 us (12%)
  between operations  0.73 us (1%)
    ppermute x15, starting transfers between devices, swap(): return lax.ppermute(array, 'node', [(n, n ^ bits) for n in range(devices)])  15.6 us
    pallas_call x2, Pallas kernels, ffn(): pl.pallas_call(functools.partial(ffn_kernel, blocks), out_shape=[jax.Shap...  9.5 us
    ppermute x2, waiting for transfers between devices, shift(): lax.ppermute(array, 'node', [(n, (n + step * SPLIT) % devices) for n in r...  8.05 us
    ppermute x15, waiting for transfers between devices, swap(): return lax.ppermute(array, 'node', [(n, n ^ bits) for n in range(devices)])  7.68 us
    unnamed x18, local copies, waits for them, and re-layouts  6.55 us
    ppermute x2, starting transfers between devices, shift(): lax.ppermute(array, 'node', [(n, (n + step * SPLIT) % devices) for n in r...  6.03 us
    pallas_call x1, Pallas kernels, finish(): pl.pallas_call(functools.partial(finish_kernel, flight, capacity), out_sh...  1.57 us
  transfers between devices with their start and end apart: 17, of which 5 were waited for; matrix products, arithmetic and copies ran while one was open for 0% of the time, Pallas kernels for 18%

profile of v1, /device:TPU:0, one launch (start us, length us, event | category | flops | bytes accessed | tf_op | source)
XLA Modules:
  0.0 56.5 jit_solution(14696141224696927685)
XLA Ops:
  0.0 0.0 copy-start
  0.0 0.5 collective-permute-start.3
  0.5 0.1 collective-permute-start.4
  0.6 0.4 collective-permute-start.5
  1.7 0.0 copy-start.5
  1.7 1.5 %copy-done.5 = bf16[128,7168]{1,0:T(8,128)(2,1)S(1)} copy-done((bf16[128,7168]{1,0:T(8,128)(2,1)S(1)}, bf16[128,7168]{1,0:T(8,128)(2,1)}, u32[]{:S(2)}) %copy-start.5) | copy-done | bytes 1835032
  3.2 0.0 copy-start.6
  3.2 0.7 %copy-done.6 = s32[128,8]{0,1:T(8,128)S(1)} copy-done((s32[128,8]{0,1:T(8,128)S(1)}, s32[128,8]{0,1:T(8,128)}, u32[]{:S(2)}) %copy-start.6) | copy-done | bytes 4120
  3.9 0.0 copy-start.7
  3.9 0.7 %copy-done.7 = s32[128,8]{0,1:T(8,128)S(1)} copy-done((s32[128,8]{0,1:T(8,128)S(1)}, s32[128,8]{0,1:T(8,128)}, u32[]{:S(2)}) %copy-start.7) | copy-done | bytes 4120
  4.5 0.0 copy-start.8
  4.5 0.7 %copy-done.8 = s32[128,4]{0,1:T(4,128)S(1)} copy-done((s32[128,4]{0,1:T(4,128)S(1)}, s32[128,4]{0,1:T(4,128)}, u32[]{:S(2)}) %copy-start.8) | copy-done | bytes 2072
  5.2 0.7 %route.1 = (bf16[8,7168]{1,0:T(8,128)(2,1)S(1)}, bf16[8,7168]{1,0:T(8,128)(2,1)S(1)}, bf16[16,128]{1,0:T(8,128)(2,1)S(1)}, f32[16,128]{1,0:T(8,128)S(1)}) custom-call(s32[1]{0:T(128)} %bitcast.me_ref, s32[1]{0:T(128)S(6)} %copy.9.count_ref, s32[4,128]{1,0:T(4,128)S(1)} %bitcast.6, s32[8,128]{1,0:T(8,128)S(1)} %bitcast.4, s32[8,128]{1,0:T(8,128)S(1)} %bitcast.5, ...), custom_call_target="tpu_custom_call" | custom-call | flops 29360128 | bytes 1835008 | tf_op jit(solution)/shard_map/route/pallas_call | solution.py:92
  5.9 3.7 %collective-permute-start.9 = (bf16[8,7168]{1,0:T(8,128)(2,1)S(1)}, bf16[8,7168]{1,0:T(8,128)(2,1)S(1)}, u32[]{:S(2)}, u32[]{:S(2)}) collective-permute-start(bf16[8,7168]{1,0:T(8,128)(2,1)S(1)} %get-tuple-element.24), channel_id=1, source_target_pairs={{0,8},{1,9},{2,10},{3,11},{4,12},{5,13},{6,14},{7,15},{8,0},{9,1},... | collective-permute-start | bytes 344072 | tf_op jit(solution)/shard_map/ppermute | solution.py:234
  9.6 6.2 %collective-permute-done.9.refs_0_ = bf16[8,7168]{1,0:T(8,128)(2,1)S(1)} collective-permute-done((bf16[8,7168]{1,0:T(8,128)(2,1)S(1)}, bf16[8,7168]{1,0:T(8,128)(2,1)S(1)}, u32[]{:S(2)}, u32[]{:S(2)}) %collective-permute-start.9) | collective-permute-done | bytes 114720 | tf_op jit(solution)/shard_map/ppermute | solution.py:234
  15.8 1.6 %collective-permute-start.10 = (bf16[8,7168]{1,0:T(8,128)(2,1)S(1)}, bf16[8,7168]{1,0:T(8,128)(2,1)S(1)}, u32[]{:S(2)}, u32[]{:S(2)}) collective-permute-start(bf16[8,7168]{1,0:T(8,128)(2,1)S(1)} %collective-permute-done.9.refs_0_), channel_id=1, source_target_pairs={{0,2},{1,3},{2,0},{3,1},{4,6},{5,7},{6,4},{7,5},{8,10},{9,11},{10,... | collective-permute-start | bytes 344072 | tf_op jit(solution)/shard_map/ppermute | solution.py:231
  17.4 0.7 %collective-permute-start.11 = (bf16[8,7168]{1,0:T(8,128)(2,1)S(1)}, bf16[8,7168]{1,0:T(8,128)(2,1)S(1)}, u32[]{:S(2)}, u32[]{:S(2)}) collective-permute-start(bf16[8,7168]{1,0:T(8,128)(2,1)S(1)} %collective-permute-done.9.refs_0_), channel_id=1, source_target_pairs={{0,4},{1,5},{2,6},{3,7},{4,0},{5,1},{6,2},{7,3},{8,12},{9,13},{10,... | collective-permute-start | bytes 344072 | tf_op jit(solution)/shard_map/ppermute | solution.py:231
  18.1 2.7 %collective-permute-done.10.refs_1_ = bf16[8,7168]{1,0:T(8,128)(2,1)S(1)} collective-permute-done((bf16[8,7168]{1,0:T(8,128)(2,1)S(1)}, bf16[8,7168]{1,0:T(8,128)(2,1)S(1)}, u32[]{:S(2)}, u32[]{:S(2)}) %collective-permute-start.10) | collective-permute-done | bytes 114720 | tf_op jit(solution)/shard_map/ppermute | solution.py:231
  20.8 1.9 %collective-permute-start.12 = (bf16[8,7168]{1,0:T(8,128)(2,1)S(1)}, bf16[8,7168]{1,0:T(8,128)(2,1)S(1)}, u32[]{:S(2)}, u32[]{:S(2)}) collective-permute-start(bf16[8,7168]{1,0:T(8,128)(2,1)S(1)} %collective-permute-done.9.refs_0_), channel_id=1, source_target_pairs={{0,6},{1,7},{2,4},{3,5},{4,2},{5,3},{6,0},{7,1},{8,14},{9,15},{10,... | collective-permute-start | bytes 344072 | tf_op jit(solution)/shard_map/ppermute | solution.py:231
  22.6 0.0 collective-permute-done.11.refs_2_
  22.6 0.5 collective-permute-start
  23.2 3.4 %collective-permute-done.12.refs_3_ = bf16[8,7168]{1,0:T(8,128)(2,1)S(1)} collective-permute-done((bf16[8,7168]{1,0:T(8,128)(2,1)S(1)}, bf16[8,7168]{1,0:T(8,128)(2,1)S(1)}, u32[]{:S(2)}, u32[]{:S(2)}) %collective-permute-start.12) | collective-permute-done | bytes 114720 | tf_op jit(solution)/shard_map/ppermute | solution.py:231
  26.6 0.9 %collective-permute-start.1 = (bf16[8,7168]{1,0:T(8,128)(2,1)S(1)}, bf16[8,7168]{1,0:T(8,128)(2,1)S(1)}, u32[]{:S(2)}, u32[]{:S(2)}) collective-permute-start(bf16[8,7168]{1,0:T(8,128)(2,1)S(1)} %get-tuple-element.19.refs_0_), channel_id=1, source_target_pairs={{0,4},{1,5},{2,6},{3,7},{4,0},{5,1},{6,2},{7,3},{8,12},{9,13},{10,... | collective-permute-start | bytes 344072 | tf_op jit(solution)/shard_map/ppermute | solution.py:231
  27.5 0.0 collective-permute-done.3.refs_5_
  27.5 2.0 %collective-permute-start.2 = (bf16[8,7168]{1,0:T(8,128)(2,1)S(1)}, bf16[8,7168]{1,0:T(8,128)(2,1)S(1)}, u32[]{:S(2)}, u32[]{:S(2)}) collective-permute-start(bf16[8,7168]{1,0:T(8,128)(2,1)S(1)} %get-tuple-element.19.refs_0_), channel_id=1, source_target_pairs={{0,6},{1,7},{2,4},{3,5},{4,2},{5,3},{6,0},{7,1},{8,14},{9,15},{10,... | collective-permute-start | bytes 344072 | tf_op jit(solution)/shard_map/ppermute | solution.py:231
  29.5 0.0 collective-permute-done.4.refs_7_
  29.5 0.0 collective-permute-done.5.refs_9_
  29.5 0.0 copy-done
  29.5 0.0 copy-start.1
  29.5 1.5 %copy-done.1 = bf16[7168,128]{1,0:T(8,128)(2,1)S(1)} copy-done((bf16[7168,128]{1,0:T(8,128)(2,1)S(1)}, bf16[7168,128]{1,0:T(8,128)(2,1)}, u32[]{:S(2)}) %copy-start.1) | copy-done | bytes 1835032
  31.0 0.0 copy-start.3
  31.0 1.5 %copy-done.3 = bf16[128,7168]{1,0:T(8,128)(2,1)S(1)} copy-done((bf16[128,7168]{1,0:T(8,128)(2,1)S(1)}, bf16[128,7168]{1,0:T(8,128)(2,1)}, u32[]{:S(2)}) %copy-start.3) | copy-done | bytes 1835032
  32.5 0.0 copy-start.2
  32.5 0.0 copy-start.4
  32.5 4.8 %ffn.3 = (bf16[8,7168]{1,0:T(8,128)(2,1)S(1)}, bf16[8,7168]{1,0:T(8,128)(2,1)S(1)}, bf16[8,7168]{1,0:T(8,128)(2,1)S(1)}, bf16[8,7168]{1,0:T(8,128)(2,1)S(1)}) custom-call(bf16[8,7168]{1,0:T(8,128)(2,1)S(1)} %collective-permute-done.9.refs_0_, bf16[8,7168]{1,0:T(8,128)(2,1)S(1)} %collective-permute-done.10.refs_1_, ...), custom_call_target="tpu_custom_call" | custom-call | flops 352321536 | bytes 11010048 | tf_op jit(solution)/shard_map/ffn/pallas_call | solution.py:148
  37.3 0.6 %collective-permute-start.13 = (bf16[8,7168]{1,0:T(8,128)(2,1)S(1)}, bf16[8,7168]{1,0:T(8,128)(2,1)S(1)}, u32[]{:S(2)}, u32[]{:S(2)}) collective-permute-start(bf16[8,7168]{1,0:T(8,128)(2,1)S(1)} %get-tuple-element.26), channel_id=1, source_target_pairs={{0,2},{1,3},{2,0},{3,1},{4,6},{5,7},{6,4},{7,5},{8,10},{9,11},{10,... | collective-permute-start | bytes 344072 | tf_op jit(solution)/shard_map/ppermute | solution.py:231
  37.9 0.9 %collective-permute-start.14 = (bf16[8,7168]{1,0:T(8,128)(2,1)S(1)}, bf16[8,7168]{1,0:T(8,128)(2,1)S(1)}, u32[]{:S(2)}, u32[]{:S(2)}) collective-permute-start(bf16[8,7168]{1,0:T(8,128)(2,1)S(1)} %get-tuple-element.27), channel_id=1, source_target_pairs={{0,4},{1,5},{2,6},{3,7},{4,0},{5,1},{6,2},{7,3},{8,12},{9,13},{10,... | collective-permute-start | bytes 344072 | tf_op jit(solution)/shard_map/ppermute | solution.py:231
  38.9 0.0 collective-permute-done.refs_1_
  38.9 2.0 %collective-permute-start.15 = (bf16[8,7168]{1,0:T(8,128)(2,1)S(1)}, bf16[8,7168]{1,0:T(8,128)(2,1)S(1)}, u32[]{:S(2)}, u32[]{:S(2)}) collective-permute-start(bf16[8,7168]{1,0:T(8,128)(2,1)S(1)} %get-tuple-element.28), channel_id=1, source_target_pairs={{0,6},{1,7},{2,4},{3,5},{4,2},{5,3},{6,0},{7,1},{8,14},{9,15},{10,... | collective-permute-start | bytes 344072 | tf_op jit(solution)/shard_map/ppermute | solution.py:231
  40.9 0.0 collective-permute-done.1.refs_2_
  40.9 0.0 collective-permute-done.2.refs_3_
  40.9 0.0 copy-done.2
  40.9 0.0 copy-done.4
  40.9 4.7 %ffn.2 = (bf16[8,7168]{1,0:T(8,128)(2,1)S(1)}, bf16[8,7168]{1,0:T(8,128)(2,1)S(1)}, bf16[8,7168]{1,0:T(8,128)(2,1)S(1)}, bf16[8,7168]{1,0:T(8,128)(2,1)S(1)}) custom-call(bf16[8,7168]{1,0:T(8,128)(2,1)S(1)} %get-tuple-element.19.refs_0_, bf16[8,7168]{1,0:T(8,128)(2,1)S(1)} %collective-permute-done.refs_1_, ...), custom_call_target="tpu_custom_call" | custom-call | flops 352321536 | bytes 11010048 | tf_op jit(solution)/shard_map/ffn/pallas_call | solution.py:148
  45.6 0.6 %collective-permute-start.6 = (bf16[8,7168]{1,0:T(8,128)(2,1)S(1)}, bf16[8,7168]{1,0:T(8,128)(2,1)S(1)}, u32[]{:S(2)}, u32[]{:S(2)}) collective-permute-start(bf16[8,7168]{1,0:T(8,128)(2,1)S(1)} %get-tuple-element.21), channel_id=1, source_target_pairs={{0,2},{1,3},{2,0},{3,1},{4,6},{5,7},{6,4},{7,5},{8,10},{9,11},{10,... | collective-permute-start | bytes 344072 | tf_op jit(solution)/shard_map/ppermute | solution.py:231
  46.2 0.9 %collective-permute-start.7 = (bf16[8,7168]{1,0:T(8,128)(2,1)S(1)}, bf16[8,7168]{1,0:T(8,128)(2,1)S(1)}, u32[]{:S(2)}, u32[]{:S(2)}) collective-permute-start(bf16[8,7168]{1,0:T(8,128)(2,1)S(1)} %get-tuple-element.22), channel_id=1, source_target_pairs={{0,4},{1,5},{2,6},{3,7},{4,0},{5,1},{6,2},{7,3},{8,12},{9,13},{10,... | collective-permute-start | bytes 344072 | tf_op jit(solution)/shard_map/ppermute | solution.py:231
  47.1 0.0 collective-permute-done.13
  47.1 2.0 %collective-permute-start.8 = (bf16[8,7168]{1,0:T(8,128)(2,1)S(1)}, bf16[8,7168]{1,0:T(8,128)(2,1)S(1)}, u32[]{:S(2)}, u32[]{:S(2)}) collective-permute-start(bf16[8,7168]{1,0:T(8,128)(2,1)S(1)} %get-tuple-element.23), channel_id=1, source_target_pairs={{0,6},{1,7},{2,4},{3,5},{4,2},{5,3},{6,0},{7,1},{8,14},{9,15},{10,... | collective-permute-start | bytes 344072 | tf_op jit(solution)/shard_map/ppermute | solution.py:231
  49.1 0.0 collective-permute-done.14
  49.1 0.0 collective-permute-done.15
  49.1 0.1 add_convert_fusion
  49.2 2.3 %collective-permute-start.16 = (bf16[8,7168]{1,0:T(8,128)(2,1)S(1)}, bf16[8,7168]{1,0:T(8,128)(2,1)S(1)}, u32[]{:S(2)}, u32[]{:S(2)}) collective-permute-start(bf16[8,7168]{1,0:T(8,128)(2,1)S(1)} %add_convert_fusion), channel_id=1, source_target_pairs={{0,8},{1,9},{2,10},{3,11},{4,12},{5,13},{6,14},{7,15},{8,0},{9,1},... | collective-permute-start | bytes 344072 | tf_op jit(solution)/shard_map/ppermute | solution.py:234
  51.5 0.0 collective-permute-done.6.refs_1_
  51.5 0.0 collective-permute-done.7.refs_2_
  51.5 1.6 %collective-permute-done.8.refs_3_ = bf16[8,7168]{1,0:T(8,128)(2,1)S(1)} collective-permute-done((bf16[8,7168]{1,0:T(8,128)(2,1)S(1)}, bf16[8,7168]{1,0:T(8,128)(2,1)S(1)}, u32[]{:S(2)}, u32[]{:S(2)}) %collective-permute-start.8) | collective-permute-done | bytes 114720 | tf_op jit(solution)/shard_map/ppermute | solution.py:231
  53.1 1.8 %collective-permute-done.16.refs_4_ = bf16[8,7168]{1,0:T(8,128)(2,1)S(1)} collective-permute-done((bf16[8,7168]{1,0:T(8,128)(2,1)S(1)}, bf16[8,7168]{1,0:T(8,128)(2,1)S(1)}, u32[]{:S(2)}, u32[]{:S(2)}) %collective-permute-start.16) | collective-permute-done | bytes 114720 | tf_op jit(solution)/shard_map/ppermute | solution.py:234
  54.9 1.6 %finish.1 = bf16[128,7168]{1,0:T(8,128)(2,1)} custom-call(bf16[16,128]{1,0:T(8,128)(2,1)S(1)} %get-tuple-element.17.select_ref, f32[16,128]{1,0:T(8,128)S(1)} %get-tuple-element.18.share_ref, bf16[8,7168]{1,0:T(8,128)(2,1)S(1)} %get-tuple-element.20.refs_0_, bf16[8,7168]{1,0:T(8,128)(2,1)S(1)} %collective-permute-done.6.refs_1_, ...), custom_call_target="tpu_custom_call" | custom-call | flops 29360128 | bytes 1835008 | tf_op jit(solution)/shard_map/finish/pallas_call | solution.py:195
Async XLA Ops:
  0.0 29.5 %copy-start = (bf16[7168,128]{1,0:T(8,128)(2,1)S(1)}, bf16[7168,128]{1,0:T(8,128)(2,1)}, u32[]{:S(2)}) copy-start(bf16[7168,128]{1,0:T(8,128)(2,1)} %refs_4_.3) | copy-start | bytes 5505028
  0.0 27.5 %collective-permute-start.3 = (bf16[7168,128]{1,0:T(8,128)(2,1)}, bf16[7168,128]{1,0:T(8,128)(2,1)}, u32[]{:S(2)}, u32[]{:S(2)}) collective-permute-start(bf16[7168,128]{1,0:T(8,128)(2,1)} %refs_4_.3), channel_id=1, source_target_pairs={{0,1},{1,0},{2,3},{3,2},{4,5},{5,4},{6,7},{7,6},{8,9},{9,8},{10,11... | collective-permute-start | bytes 5505032 | tf_op jit(solution)/shard_map/ppermute | solution.py:231
  0.5 29.0 %collective-permute-start.4 = (bf16[7168,128]{1,0:T(8,128)(2,1)}, bf16[7168,128]{1,0:T(8,128)(2,1)}, u32[]{:S(2)}, u32[]{:S(2)}) collective-permute-start(bf16[7168,128]{1,0:T(8,128)(2,1)} %refs_6_.3), channel_id=1, source_target_pairs={{0,1},{1,0},{2,3},{3,2},{4,5},{5,4},{6,7},{7,6},{8,9},{9,8},{10,11... | collective-permute-start | bytes 5505032 | tf_op jit(solution)/shard_map/ppermute | solution.py:231
  0.6 28.9 %collective-permute-start.5 = (bf16[128,7168]{1,0:T(8,128)(2,1)}, bf16[128,7168]{1,0:T(8,128)(2,1)}, u32[]{:S(2)}, u32[]{:S(2)}) collective-permute-start(bf16[128,7168]{1,0:T(8,128)(2,1)} %refs_8_.3), channel_id=1, source_target_pairs={{0,1},{1,0},{2,3},{3,2},{4,5},{5,4},{6,7},{7,6},{8,9},{9,8},{10,11... | collective-permute-start | bytes 5505032 | tf_op jit(solution)/shard_map/ppermute | solution.py:231
  1.7 1.5 %copy-start.5 = (bf16[128,7168]{1,0:T(8,128)(2,1)S(1)}, bf16[128,7168]{1,0:T(8,128)(2,1)}, u32[]{:S(2)}) copy-start(bf16[128,7168]{1,0:T(8,128)(2,1)} %tokens_ref.1) | copy-start | bytes 5505028
  3.2 0.7 %copy-start.6 = (s32[128,8]{0,1:T(8,128)S(1)}, s32[128,8]{0,1:T(8,128)}, u32[]{:S(2)}) copy-start(s32[128,8]{0,1:T(8,128)} %param.10) | copy-start | bytes 12292
  3.9 0.7 %copy-start.7 = (s32[128,8]{0,1:T(8,128)S(1)}, s32[128,8]{0,1:T(8,128)}, u32[]{:S(2)}) copy-start(s32[128,8]{0,1:T(8,128)} %param.11) | copy-start | bytes 12292
  4.5 0.7 %copy-start.8 = (s32[128,4]{0,1:T(4,128)S(1)}, s32[128,4]{0,1:T(4,128)}, u32[]{:S(2)}) copy-start(s32[128,4]{0,1:T(4,128)} %param.9) | copy-start | bytes 6148
  5.9 9.9 %collective-permute-start.9 = (bf16[8,7168]{1,0:T(8,128)(2,1)S(1)}, bf16[8,7168]{1,0:T(8,128)(2,1)S(1)}, u32[]{:S(2)}, u32[]{:S(2)}) collective-permute-start(bf16[8,7168]{1,0:T(8,128)(2,1)S(1)} %get-tuple-element.24), channel_id=1, source_target_pairs={{0,8},{1,9},{2,10},{3,11},{4,12},{5,13},{6,14},{7,15},{8,0},{9,1},... | collective-permute-start | bytes 344072 | tf_op jit(solution)/shard_map/ppermute | solution.py:234
  15.8 4.9 %collective-permute-start.10 = (bf16[8,7168]{1,0:T(8,128)(2,1)S(1)}, bf16[8,7168]{1,0:T(8,128)(2,1)S(1)}, u32[]{:S(2)}, u32[]{:S(2)}) collective-permute-start(bf16[8,7168]{1,0:T(8,128)(2,1)S(1)} %collective-permute-done.9.refs_0_), channel_id=1, source_target_pairs={{0,2},{1,3},{2,0},{3,1},{4,6},{5,7},{6,4},{7,5},{8,10},{9,11},{10,... | collective-permute-start | bytes 344072 | tf_op jit(solution)/shard_map/ppermute | solution.py:231
  17.4 5.2 %collective-permute-start.11 = (bf16[8,7168]{1,0:T(8,128)(2,1)S(1)}, bf16[8,7168]{1,0:T(8,128)(2,1)S(1)}, u32[]{:S(2)}, u32[]{:S(2)}) collective-permute-start(bf16[8,7168]{1,0:T(8,128)(2,1)S(1)} %collective-permute-done.9.refs_0_), channel_id=1, source_target_pairs={{0,4},{1,5},{2,6},{3,7},{4,0},{5,1},{6,2},{7,3},{8,12},{9,13},{10,... | collective-permute-start | bytes 344072 | tf_op jit(solution)/shard_map/ppermute | solution.py:231
  20.8 5.8 %collective-permute-start.12 = (bf16[8,7168]{1,0:T(8,128)(2,1)S(1)}, bf16[8,7168]{1,0:T(8,128)(2,1)S(1)}, u32[]{:S(2)}, u32[]{:S(2)}) collective-permute-start(bf16[8,7168]{1,0:T(8,128)(2,1)S(1)} %collective-permute-done.9.refs_0_), channel_id=1, source_target_pairs={{0,6},{1,7},{2,4},{3,5},{4,2},{5,3},{6,0},{7,1},{8,14},{9,15},{10,... | collective-permute-start | bytes 344072 | tf_op jit(solution)/shard_map/ppermute | solution.py:231
  22.6 16.2 %collective-permute-start = (bf16[8,7168]{1,0:T(8,128)(2,1)S(1)}, bf16[8,7168]{1,0:T(8,128)(2,1)S(1)}, u32[]{:S(2)}, u32[]{:S(2)}) collective-permute-start(bf16[8,7168]{1,0:T(8,128)(2,1)S(1)} %get-tuple-element.19.refs_0_), channel_id=1, source_target_pairs={{0,2},{1,3},{2,0},{3,1},{4,6},{5,7},{6,4},{7,5},{8,10},{9,11},{10,... | collective-permute-start | bytes 344072 | tf_op jit(solution)/shard_map/ppermute | solution.py:231
  26.6 14.3 %collective-permute-start.1 = (bf16[8,7168]{1,0:T(8,128)(2,1)S(1)}, bf16[8,7168]{1,0:T(8,128)(2,1)S(1)}, u32[]{:S(2)}, u32[]{:S(2)}) collective-permute-start(bf16[8,7168]{1,0:T(8,128)(2,1)S(1)} %get-tuple-element.19.refs_0_), channel_id=1, source_target_pairs={{0,4},{1,5},{2,6},{3,7},{4,0},{5,1},{6,2},{7,3},{8,12},{9,13},{10,... | collective-permute-start | bytes 344072 | tf_op jit(solution)/shard_map/ppermute | solution.py:231
  27.5 13.4 %collective-permute-start.2 = (bf16[8,7168]{1,0:T(8,128)(2,1)S(1)}, bf16[8,7168]{1,0:T(8,128)(2,1)S(1)}, u32[]{:S(2)}, u32[]{:S(2)}) collective-permute-start(bf16[8,7168]{1,0:T(8,128)(2,1)S(1)} %get-tuple-element.19.refs_0_), channel_id=1, source_target_pairs={{0,6},{1,7},{2,4},{3,5},{4,2},{5,3},{6,0},{7,1},{8,14},{9,15},{10,... | collective-permute-start | bytes 344072 | tf_op jit(solution)/shard_map/ppermute | solution.py:231
  29.5 1.5 %copy-start.1 = (bf16[7168,128]{1,0:T(8,128)(2,1)S(1)}, bf16[7168,128]{1,0:T(8,128)(2,1)}, u32[]{:S(2)}) copy-start(bf16[7168,128]{1,0:T(8,128)(2,1)} %refs_6_.3) | copy-start | bytes 5505028
  31.0 1.5 %copy-start.3 = (bf16[128,7168]{1,0:T(8,128)(2,1)S(1)}, bf16[128,7168]{1,0:T(8,128)(2,1)}, u32[]{:S(2)}) copy-start(bf16[128,7168]{1,0:T(8,128)(2,1)} %refs_8_.3) | copy-start | bytes 5505028
  32.5 8.4 %copy-start.2 = (bf16[7168,128]{1,0:T(8,128)(2,1)S(1)}, bf16[7168,128]{1,0:T(8,128)(2,1)}, u32[]{:S(2)}) copy-start(bf16[7168,128]{1,0:T(8,128)(2,1)} %refs_6_.3) | copy-start | bytes 5505028
  32.5 8.4 %copy-start.4 = (bf16[128,7168]{1,0:T(8,128)(2,1)S(1)}, bf16[128,7168]{1,0:T(8,128)(2,1)}, u32[]{:S(2)}) copy-start(bf16[128,7168]{1,0:T(8,128)(2,1)} %refs_8_.3) | copy-start | bytes 5505028
  37.3 9.8 %collective-permute-start.13 = (bf16[8,7168]{1,0:T(8,128)(2,1)S(1)}, bf16[8,7168]{1,0:T(8,128)(2,1)S(1)}, u32[]{:S(2)}, u32[]{:S(2)}) collective-permute-start(bf16[8,7168]{1,0:T(8,128)(2,1)S(1)} %get-tuple-element.26), channel_id=1, source_target_pairs={{0,2},{1,3},{2,0},{3,1},{4,6},{5,7},{6,4},{7,5},{8,10},{9,11},{10,... | collective-permute-start | bytes 344072 | tf_op jit(solution)/shard_map/ppermute | solution.py:231
  37.9 11.2 %collective-permute-start.14 = (bf16[8,7168]{1,0:T(8,128)(2,1)S(1)}, bf16[8,7168]{1,0:T(8,128)(2,1)S(1)}, u32[]{:S(2)}, u32[]{:S(2)}) collective-permute-start(bf16[8,7168]{1,0:T(8,128)(2,1)S(1)} %get-tuple-element.27), channel_id=1, source_target_pairs={{0,4},{1,5},{2,6},{3,7},{4,0},{5,1},{6,2},{7,3},{8,12},{9,13},{10,... | collective-permute-start | bytes 344072 | tf_op jit(solution)/shard_map/ppermute | solution.py:231
  38.9 10.2 %collective-permute-start.15 = (bf16[8,7168]{1,0:T(8,128)(2,1)S(1)}, bf16[8,7168]{1,0:T(8,128)(2,1)S(1)}, u32[]{:S(2)}, u32[]{:S(2)}) collective-permute-start(bf16[8,7168]{1,0:T(8,128)(2,1)S(1)} %get-tuple-element.28), channel_id=1, source_target_pairs={{0,6},{1,7},{2,4},{3,5},{4,2},{5,3},{6,0},{7,1},{8,14},{9,15},{10,... | collective-permute-start | bytes 344072 | tf_op jit(solution)/shard_map/ppermute | solution.py:231
  45.6 5.9 %collective-permute-start.6 = (bf16[8,7168]{1,0:T(8,128)(2,1)S(1)}, bf16[8,7168]{1,0:T(8,128)(2,1)S(1)}, u32[]{:S(2)}, u32[]{:S(2)}) collective-permute-start(bf16[8,7168]{1,0:T(8,128)(2,1)S(1)} %get-tuple-element.21), channel_id=1, source_target_pairs={{0,2},{1,3},{2,0},{3,1},{4,6},{5,7},{6,4},{7,5},{8,10},{9,11},{10,... | collective-permute-start | bytes 344072 | tf_op jit(solution)/shard_map/ppermute | solution.py:231
  46.2 5.3 %collective-permute-start.7 = (bf16[8,7168]{1,0:T(8,128)(2,1)S(1)}, bf16[8,7168]{1,0:T(8,128)(2,1)S(1)}, u32[]{:S(2)}, u32[]{:S(2)}) collective-permute-start(bf16[8,7168]{1,0:T(8,128)(2,1)S(1)} %get-tuple-element.22), channel_id=1, source_target_pairs={{0,4},{1,5},{2,6},{3,7},{4,0},{5,1},{6,2},{7,3},{8,12},{9,13},{10,... | collective-permute-start | bytes 344072 | tf_op jit(solution)/shard_map/ppermute | solution.py:231
  47.1 6.0 %collective-permute-start.8 = (bf16[8,7168]{1,0:T(8,128)(2,1)S(1)}, bf16[8,7168]{1,0:T(8,128)(2,1)S(1)}, u32[]{:S(2)}, u32[]{:S(2)}) collective-permute-start(bf16[8,7168]{1,0:T(8,128)(2,1)S(1)} %get-tuple-element.23), channel_id=1, source_target_pairs={{0,6},{1,7},{2,4},{3,5},{4,2},{5,3},{6,0},{7,1},{8,14},{9,15},{10,... | collective-permute-start | bytes 344072 | tf_op jit(solution)/shard_map/ppermute | solution.py:231
  49.2 5.8 %collective-permute-start.16 = (bf16[8,7168]{1,0:T(8,128)(2,1)S(1)}, bf16[8,7168]{1,0:T(8,128)(2,1)S(1)}, u32[]{:S(2)}, u32[]{:S(2)}) collective-permute-start(bf16[8,7168]{1,0:T(8,128)(2,1)S(1)} %add_convert_fusion), channel_id=1, source_target_pairs={{0,8},{1,9},{2,10},{3,11},{4,12},{5,13},{6,14},{7,15},{8,0},{9,1},... | collective-permute-start | bytes 344072 | tf_op jit(solution)/shard_map/ppermute | solution.py:234
